TPU v7x, 32 devices: a whole 2x2x4 slice. The times are simulated.
32 devices in a mesh: section: 4 (over x, core), kv: 8 (over z, y).
Axes of the slice: x: 2, y: 2, z: 4, core: 2. Of those that a mesh axis runs over, the one named last changes fastest.
Arguments:
- queries: bfloat16 [256, 8192], P(('section', 'kv')), may hold values from -72 to 72
- new_keys: bfloat16 [256, 1024], P(('section', 'kv')), may hold values from -6 to 6
- new_values: bfloat16 [256, 1024], P(('section', 'kv')), may hold values from -6 to 6
- prefix_keys: bfloat16 [32768, 1024], P(('section', 'kv')), may hold values from -20 to 20
- prefix_values: bfloat16 [32768, 1024], P(('section', 'kv')), may hold values from -6 to 6
- lengths: int32 [4], replicated, may hold values from 512 to 8192, as said below
Outputs:
- attended: bfloat16 [256, 8192], P(('section', 'kv'))
Inputs may be any that keep to these rules, and one draw needn't show every extreme that they name: `lengths`: some section has 8192 live rows and another 8192 // 16.
All inputs are finite; a program needn't handle non-finite values.
Results may differ from a plain program's by a relative error of at most 0.005.
Values may be sent and summed in bfloat16 or wider, within the bound.
A program may use at most 256 MiB of HBM per device.

v0:
```python
import functools

import jax
import jax.numpy as jnp
from jax import lax
from jax.experimental import pallas as pl
from jax.experimental.pallas import tpu as pltpu
from jax.sharding import PartitionSpec as P

H = 64
KVH = 8
DH = 128
G = H // KVH
LANES = 128
NEG = -1e30
HALVES = 2
LAG = 2
LOG2E = 1.4426950408889634
MESH = pl.DeviceIdType.MESH
F32 = jnp.float32
BF16 = jnp.bfloat16


def lane_of(stats, h):
    return jnp.broadcast_to(stats[:, h : h + 1], stats.shape)


def kernel(
    sections, outer, inner,
    lengths_ref, q_hbm, nk_hbm, nv_hbm, k_hbm, v_hbm, out_ref,
    nkbuf, nvbuf, kbuf, vbuf, qbuf, obuf, ostat, ybuf, ystat, cbuf, cstat, zbuf, zstat,
    local_sem, qz_send, qy_send, qf_send, q_recv,
    yo_send, ys_send, yo_recv, ys_recv, zo_send, zs_send, zo_recv, zs_recv,
):
    sec = lax.axis_index("section")
    me = lax.axis_index("kv")
    a = me // inner
    b = me % inner
    following = (sec + 1) % sections
    previous = (sec + sections - 1) % sections
    rows = q_hbm.shape[0]
    depth = k_hbm.shape[0]
    span = q_hbm.shape[1] // HALVES
    heads = H // HALVES

    def cut(hf):
        return pl.ds(hf * span, span)

    def outer_at(d):
        return (a + d) % outer

    def outer_back(d):
        return (a + outer - d) % outer

    def inner_at(e):
        return (b + e) % inner

    loads = [
        pltpu.make_async_copy(k_hbm, kbuf.at[pl.ds(0, depth)], local_sem.at[0]),
        pltpu.make_async_copy(v_hbm, vbuf.at[pl.ds(0, depth)], local_sem.at[1]),
        pltpu.make_async_copy(q_hbm, qbuf.at[me], local_sem.at[2]),
        pltpu.make_async_copy(nk_hbm, nkbuf, local_sem.at[3]),
        pltpu.make_async_copy(nv_hbm, nvbuf, local_sem.at[4]),
    ]
    for load in loads:
        load.start()

    barrier = pltpu.get_barrier_semaphore()
    peers = [(sec, outer_at(d) * inner + b) for d in range(1, outer)]
    peers += [(sec, a * inner + inner_at(e)) for e in range(1, inner)]
    for d in range(outer):
        peers.append((following, outer_at(d) * inner + b))
        peers.append((previous, outer_at(d) * inner + b))
    for s_at, k_at in peers:
        pl.semaphore_signal(
            barrier, inc=1, device_id={"section": s_at, "kv": k_at}, device_id_type=MESH
        )
    pl.semaphore_wait(barrier, len(peers))

    sends = []

    def push(src, dst, send_sem, recv_sem, s_at, k_at):
        copy = pltpu.make_async_remote_copy(
            src_ref=src, dst_ref=dst, send_sem=send_sem, recv_sem=recv_sem,
            device_id={"section": s_at, "kv": k_at}, device_id_type=MESH,
        )
        copy.start()
        sends.append(copy)

    def arrived(dst, recv_sem):
        pltpu.make_async_copy(dst, dst, recv_sem).wait()

    for hf in range(HALVES):
        for e in range(1, inner):
            push(
                q_hbm.at[:, cut(hf)], qbuf.at[me, :, cut(hf)], qy_send.at[e, hf], q_recv.at[me, hf],
                sec, a * inner + inner_at(e),
            )
    for d in range(1, outer):
        for hf in range(HALVES):
            push(
                q_hbm.at[:, cut(hf)], qbuf.at[me, :, cut(hf)], qz_send.at[d, hf], q_recv.at[me, hf],
                sec, outer_at(d) * inner + b,
            )

    def forward(d, hf):
        slot = outer_back(d) * inner + b
        piece = qbuf.at[slot, :, cut(hf)]
        arrived(piece, q_recv.at[slot, hf])
        for e in range(1, inner):
            push(
                piece, piece, qf_send.at[d, e, hf], q_recv.at[slot, hf], sec, a * inner + inner_at(e)
            )

    limit = lengths_ref[sec] - me * depth
    place = lax.broadcasted_iota(jnp.int32, (1, depth), 1)
    bias = jnp.where(place < limit, 0.0, NEG).astype(F32)
    scale = (DH ** -0.5) * LOG2E
    count = inner * G * rows
    lane = lax.broadcasted_iota(jnp.int32, (rows, LANES), 1)
    sub = lax.broadcasted_iota(jnp.int32, (rows, LANES), 0)
    ones = jnp.ones((depth + LANES, LANES), BF16)

    def compute(zc, hf):
        own_bias = jnp.concatenate(
            [
                jnp.where(
                    (lane < rows) & (me * rows + lane <= (zc * inner + y) * rows + sub), 0.0, NEG
                ).astype(F32)
                for y in range(inner)
                for _ in range(G)
            ],
            0,
        )

        def one_head(g, stats):
            at = pl.multiple_of(g * DH, DH)
            k = kbuf[:, pl.ds(at, DH)]
            v = vbuf[:, pl.ds(at, DH)]
            q = jnp.concatenate(
                [
                    qbuf[zc * inner + y, :, pl.ds(pl.multiple_of(g * G * DH + h * DH, DH), DH)].astype(F32)
                    for y in range(inner)
                    for h in range(G)
                ],
                0,
            ).astype(BF16)
            s = lax.dot_general(q, k, (((1,), (1,)), ((), ())), preferred_element_type=F32) * scale
            s_old = s[:, :depth] + bias
            s_own = s[:, depth:] + own_bias
            peak = jnp.maximum(
                jnp.max(s_old, axis=-1, keepdims=True), jnp.max(s_own, axis=-1, keepdims=True)
            )
            p = jnp.concatenate([jnp.exp2(s_old - peak), jnp.exp2(s_own - peak)], 1).astype(BF16)
            acc = jnp.dot(p, jnp.concatenate([v, ones], 1), preferred_element_type=F32)
            total = acc[:, DH:]
            o = acc[:, :DH] / total
            level = peak + jnp.log2(total)
            stats = list(stats)
            for y in range(inner):
                for h in range(G):
                    base = (y * G + h) * rows
                    obuf[zc * inner + y, :, pl.ds(pl.multiple_of(g * G * DH + h * DH, DH), DH)] = o[
                        base : base + rows
                    ].astype(BF16)
                    stats[y] = jnp.where(lane == g * G + h, level[base : base + rows], stats[y])
            return tuple(stats)

        stats = lax.fori_loop(
            hf * (KVH // HALVES), (hf + 1) * (KVH // HALVES), one_head,
            tuple(jnp.zeros((rows, LANES), F32) for _ in range(inner)), unroll=2
        )
        for y in range(inner):
            ostat[zc * inner + y, hf] = stats[y]

    def spread(zc, hf):
        for e in range(1, inner):
            target = a * inner + inner_at(e)
            slot = zc * inner + inner_at(e)
            push(
                obuf.at[slot, :, cut(hf)], ybuf.at[zc, b, :, cut(hf)],
                yo_send.at[zc, inner_at(e), hf], yo_recv.at[zc, b, hf], sec, target,
            )
            push(
                ostat.at[slot, hf], ystat.at[zc, b, hf],
                ys_send.at[zc, inner_at(e), hf], ys_recv.at[zc, b, hf], sec, target,
            )

    def mix(hf, parts, levels, store):
        peak = functools.reduce(jnp.maximum, levels)
        shares = [jnp.exp2(level - peak) for level in levels]
        total = functools.reduce(jnp.add, shares)
        shares = [share / total for share in shares]
        for h in range(hf * heads, (hf + 1) * heads):
            cols = pl.ds(h * DH, DH)
            value = functools.reduce(
                jnp.add,
                [part[:, cols].astype(F32) * lane_of(share, h) for part, share in zip(parts, shares)],
            )
            store(cols, value.astype(BF16))
        return peak + jnp.log2(total)

    def combine(zc, hf):
        parts, levels = [obuf.at[zc * inner + b]], [ostat[zc * inner + b, hf]]
        for e in range(1, inner):
            at = inner_at(e)
            arrived(ybuf.at[zc, at, :, cut(hf)], yo_recv.at[zc, at, hf])
            arrived(ystat.at[zc, at, hf], ys_recv.at[zc, at, hf])
            parts.append(ybuf.at[zc, at])
            levels.append(ystat[zc, at, hf])

        def store(cols, value):
            cbuf[zc, :, cols] = value

        cstat[zc, hf] = mix(hf, parts, levels, store)
        target = zc * inner + b
        push(
            cbuf.at[zc, :, cut(hf)], zbuf.at[a, :, cut(hf)], zo_send.at[zc, hf], zo_recv.at[a, hf],
            following, target,
        )
        push(
            cstat.at[zc, hf], zstat.at[a, hf], zs_send.at[zc, hf], zs_recv.at[a, hf],
            following, target,
        )

    for load in loads:
        load.wait()
    pad = jnp.zeros((LANES - rows, kbuf.shape[1]), F32)
    kbuf[pl.ds(depth, LANES), :] = jnp.concatenate([nkbuf[...].astype(F32), pad], 0).astype(BF16)
    vbuf[pl.ds(depth, LANES), :] = jnp.concatenate([nvbuf[...].astype(F32), pad], 0).astype(BF16)
    steps = [(d, hf) for d in range(outer) for hf in range(HALVES)]
    for t, (d, hf) in enumerate(steps):
        zc = outer_back(d)
        if d + 1 < outer:
            forward(d + 1, hf)
        for e in range(1, inner):
            slot = zc * inner + inner_at(e)
            arrived(qbuf.at[slot, :, cut(hf)], q_recv.at[slot, hf])
        compute(zc, hf)
        spread(zc, hf)
        if t >= LAG:
            combine(outer_back(steps[t - LAG][0]), steps[t - LAG][1])
    for d, hf in steps[len(steps) - LAG :]:
        combine(outer_back(d), hf)

    def store_out(cols, value):
        out_ref[:, cols] = value

    for hf in range(HALVES):
        for z in range(outer):
            arrived(zbuf.at[z, :, cut(hf)], zo_recv.at[z, hf])
            arrived(zstat.at[z, hf], zs_recv.at[z, hf])
        mix(
            hf, [zbuf.at[z] for z in range(outer)], [zstat[z, hf] for z in range(outer)], store_out
        )
    for copy in sends:
        copy.wait_send()


def split_of(count):
    return 1 << ((count.bit_length() - 1) // 2)


def on_device(sections, count, queries, new_keys, new_values, prefix_keys, prefix_values, lengths):
    inner = split_of(count)
    outer = count // inner
    rows, width = queries.shape
    depth, kv_width = prefix_keys.shape
    vmem = pl.BlockSpec(memory_space=pltpu.VMEM)
    anywhere = pl.BlockSpec(memory_space=pltpu.HBM)
    dma = pltpu.SemaphoreType.DMA
    return pl.pallas_call(
        functools.partial(kernel, sections, outer, inner),
        out_shape=jax.ShapeDtypeStruct((rows, width), BF16),
        in_specs=[pl.BlockSpec(memory_space=pltpu.SMEM), anywhere, anywhere, anywhere, anywhere, anywhere],
        out_specs=vmem,
        scratch_shapes=[
            pltpu.VMEM((rows, kv_width), BF16),
            pltpu.VMEM((rows, kv_width), BF16),
            pltpu.VMEM((depth + LANES, kv_width), BF16),
            pltpu.VMEM((depth + LANES, kv_width), BF16),
            pltpu.VMEM((count, rows, width), BF16),
            pltpu.VMEM((count, rows, width), BF16),
            pltpu.VMEM((count, HALVES, rows, LANES), F32),
            pltpu.VMEM((outer, inner, rows, width), BF16),
            pltpu.VMEM((outer, inner, HALVES, rows, LANES), F32),
            pltpu.VMEM((outer, rows, width), BF16),
            pltpu.VMEM((outer, HALVES, rows, LANES), F32),
            pltpu.VMEM((outer, rows, width), BF16),
            pltpu.VMEM((outer, HALVES, rows, LANES), F32),
            dma((5,)),
            dma((outer, HALVES)),
            dma((inner, HALVES)),
            dma((outer, inner, HALVES)),
            dma((count, HALVES)),
            dma((outer, inner, HALVES)),
            dma((outer, inner, HALVES)),
            dma((outer, inner, HALVES)),
            dma((outer, inner, HALVES)),
            dma((outer, HALVES)),
            dma((outer, HALVES)),
            dma((outer, HALVES)),
            dma((outer, HALVES)),
        ],
        compiler_params=pltpu.CompilerParams(
            collective_id=0, has_side_effects=True, vmem_limit_bytes=56 << 20
        ),
        name="section_attention",
    )(lengths, queries, new_keys, new_values, prefix_keys, prefix_values)


def solution(mesh):
    return jax.shard_map(
        functools.partial(on_device, mesh.shape["section"], mesh.shape["kv"]),
        mesh=mesh,
        in_specs=(
            P(("section", "kv"), None),
            P(("section", "kv"), None),
            P(("section", "kv"), None),
            P(("section", "kv"), None),
            P(("section", "kv"), None),
            P(),
        ),
        out_specs=P(("section", "kv"), None),
        check_vma=False,
    )
```

profile of v0, /device:TPU:1, one launch (start us, length us, event | category | flops | bytes accessed | tf_op | source)
XLA Modules:
  0.0 44.5 jit_solution(5533942588563343930)
XLA Ops:
  0.0 42.9 %section_attention.1 = bf16[8,8192]{1,0:T(8,128)(2,1)} custom-call(s32[4]{0:T(128)} %lengths_ref.1, bf16[8,8192]{1,0:T(8,128)(2,1)} %q_hbm.1, bf16[8,1024]{1,0:T(8,128)(2,1)} %nk_hbm.1, bf16[8,1024]{1,0:T(8,128)(2,1)} %nv_hbm.1, bf16[1024,1024]{1,0:T(8,128)(2,1)} %k_hbm.1, bf16[1024,1024]{1,0:T(8,128)(2,1)} %v_hbm.1), custom_call_target="tpu_custom_call" | custom-call | tf_op jit(solution)/shard_map/section_attention/pallas_call | solution.py:272
  42.9 1.6 %copy.8 = bf16[8,8192]{1,0:T(8,128)(2,1)} copy(bf16[8,8192]{1,0:T(8,128)(2,1)} %section_attention.1) | data formatting | bytes 262144
where the time goes:
time: 44.6 us; the launch traced here: 44.5 us
  Pallas kernels  42.9 us (96%)
  local copies, waits for them, and re-layouts  1.57 us (4%)
    pallas_call x1, Pallas kernels, on_device(): pl.pallas_call(functools.partial(kernel, sections, outer, inner), out_sha...  42.9 us
    unnamed x1, local copies, waits for them, and re-layouts  1.57 us

commit v1 on v0

--- a/solution.py
+++ b/solution.py
@@ -14,7 +14,7 @@
 LANES = 128
 NEG = -1e30
 HALVES = 2
-LAG = 2
+LAG = 1
 LOG2E = 1.4426950408889634
 MESH = pl.DeviceIdType.MESH
 F32 = jnp.float32
@@ -30,7 +30,7 @@
     lengths_ref, q_hbm, nk_hbm, nv_hbm, k_hbm, v_hbm, out_ref,
     nkbuf, nvbuf, kbuf, vbuf, qbuf, obuf, ostat, ybuf, ystat, cbuf, cstat, zbuf, zstat,
     local_sem, qz_send, qy_send, qf_send, q_recv,
-    yo_send, ys_send, yo_recv, ys_recv, zo_send, zs_send, zo_recv, zs_recv,
+    yo_send, ys_send, yo_recv, ys_recv, xo_send, xs_send, zo_send, zs_send, zo_recv, zs_recv,
 ):
     sec = lax.axis_index("section")
     me = lax.axis_index("kv")
@@ -47,10 +47,18 @@
         return pl.ds(hf * span, span)
 
     def outer_at(d):
-        return (a + d) % outer
+        if outer & (outer - 1):
+            return (a + d) % outer
+        at, bit = 0, 1
+        while bit < outer:
+            at = at + ((a // bit + d // bit) % 2) * bit
+            bit *= 2
+        return at
 
     def outer_back(d):
-        return (a + outer - d) % outer
+        if outer & (outer - 1):
+            return (a + outer - d) % outer
+        return outer_at(d)
 
     def inner_at(e):
         return (b + e) % inner
@@ -68,9 +76,7 @@
     barrier = pltpu.get_barrier_semaphore()
     peers = [(sec, outer_at(d) * inner + b) for d in range(1, outer)]
     peers += [(sec, a * inner + inner_at(e)) for e in range(1, inner)]
-    for d in range(outer):
-        peers.append((following, outer_at(d) * inner + b))
-        peers.append((previous, outer_at(d) * inner + b))
+    peers += [(following, me), (previous, me)]
     for s_at, k_at in peers:
         pl.semaphore_signal(
             barrier, inc=1, device_id={"section": s_at, "kv": k_at}, device_id_type=MESH
@@ -145,17 +151,19 @@
                 ],
                 0,
             ).astype(BF16)
-            s = lax.dot_general(q, k, (((1,), (1,)), ((), ())), preferred_element_type=F32) * scale
+            s = lax.dot_general(q, k, (((1,), (1,)), ((), ())), preferred_element_type=F32)
             s_old = s[:, :depth] + bias
             s_own = s[:, depth:] + own_bias
             peak = jnp.maximum(
                 jnp.max(s_old, axis=-1, keepdims=True), jnp.max(s_own, axis=-1, keepdims=True)
             )
-            p = jnp.concatenate([jnp.exp2(s_old - peak), jnp.exp2(s_own - peak)], 1).astype(BF16)
+            p = jnp.concatenate(
+                [jnp.exp2((s_old - peak) * scale), jnp.exp2((s_own - peak) * scale)], 1
+            ).astype(BF16)
             acc = jnp.dot(p, jnp.concatenate([v, ones], 1), preferred_element_type=F32)
             total = acc[:, DH:]
             o = acc[:, :DH] / total
-            level = peak + jnp.log2(total)
+            level = peak * scale + jnp.log2(total)
             stats = list(stats)
             for y in range(inner):
                 for h in range(G):
@@ -168,7 +176,7 @@
 
         stats = lax.fori_loop(
             hf * (KVH // HALVES), (hf + 1) * (KVH // HALVES), one_head,
-            tuple(jnp.zeros((rows, LANES), F32) for _ in range(inner)), unroll=2
+            tuple(jnp.zeros((rows, LANES), F32) for _ in range(inner)), unroll=KVH // HALVES
         )
         for y in range(inner):
             ostat[zc * inner + y, hf] = stats[y]
@@ -184,6 +192,18 @@
             push(
                 ostat.at[slot, hf], ystat.at[zc, b, hf],
                 ys_send.at[zc, inner_at(e), hf], ys_recv.at[zc, b, hf], sec, target,
+            )
+
+    def deliver(hf):
+        for e in range(inner):
+            target = a * inner + inner_at(e)
+            push(
+                obuf.at[target, :, cut(hf)], zbuf.at[outer + b, :, cut(hf)],
+                xo_send.at[inner_at(e), hf], zo_recv.at[outer + b, hf], following, target,
+            )
+            push(
+                ostat.at[target, hf], zstat.at[outer + b, hf],
+                xs_send.at[inner_at(e), hf], zs_recv.at[outer + b, hf], following, target,
             )
 
     def mix(hf, parts, levels, store):
@@ -231,27 +251,31 @@
     steps = [(d, hf) for d in range(outer) for hf in range(HALVES)]
     for t, (d, hf) in enumerate(steps):
         zc = outer_back(d)
-        if d + 1 < outer:
-            forward(d + 1, hf)
+        if t + 1 < len(steps) and steps[t + 1][0] > 0:
+            forward(*steps[t + 1])
         for e in range(1, inner):
             slot = zc * inner + inner_at(e)
             arrived(qbuf.at[slot, :, cut(hf)], q_recv.at[slot, hf])
         compute(zc, hf)
-        spread(zc, hf)
-        if t >= LAG:
+        if d > 0:
+            spread(zc, hf)
+        if t >= LAG and steps[t - LAG][0] > 0:
             combine(outer_back(steps[t - LAG][0]), steps[t - LAG][1])
+    for hf in range(HALVES):
+        deliver(hf)
     for d, hf in steps[len(steps) - LAG :]:
         combine(outer_back(d), hf)
 
     def store_out(cols, value):
         out_ref[:, cols] = value
 
+    origins = [outer_at(d) for d in range(1, outer)] + [outer + y for y in range(inner)]
     for hf in range(HALVES):
-        for z in range(outer):
-            arrived(zbuf.at[z, :, cut(hf)], zo_recv.at[z, hf])
-            arrived(zstat.at[z, hf], zs_recv.at[z, hf])
+        for at in origins:
+            arrived(zbuf.at[at, :, cut(hf)], zo_recv.at[at, hf])
+            arrived(zstat.at[at, hf], zs_recv.at[at, hf])
         mix(
-            hf, [zbuf.at[z] for z in range(outer)], [zstat[z, hf] for z in range(outer)], store_out
+            hf, [zbuf.at[at] for at in origins], [zstat[at, hf] for at in origins], store_out
         )
     for copy in sends:
         copy.wait_send()
@@ -286,8 +310,8 @@
             pltpu.VMEM((outer, inner, HALVES, rows, LANES), F32),
             pltpu.VMEM((outer, rows, width), BF16),
             pltpu.VMEM((outer, HALVES, rows, LANES), F32),
-            pltpu.VMEM((outer, rows, width), BF16),
-            pltpu.VMEM((outer, HALVES, rows, LANES), F32),
+            pltpu.VMEM((outer + inner, rows, width), BF16),
+            pltpu.VMEM((outer + inner, HALVES, rows, LANES), F32),
             dma((5,)),
             dma((outer, HALVES)),
             dma((inner, HALVES)),
@@ -297,10 +321,12 @@
             dma((outer, inner, HALVES)),
             dma((outer, inner, HALVES)),
             dma((outer, inner, HALVES)),
+            dma((inner, HALVES)),
+            dma((inner, HALVES)),
             dma((outer, HALVES)),
             dma((outer, HALVES)),
-            dma((outer, HALVES)),
-            dma((outer, HALVES)),
+            dma((outer + inner, HALVES)),
+            dma((outer + inner, HALVES)),
         ],
         compiler_params=pltpu.CompilerParams(
             collective_id=0, has_side_effects=True, vmem_limit_bytes=56 << 20

time: 44.6 us -> 43.3 us (0.971)
  Pallas kernels: 42.9 us -> 41.5 us
    pallas_call x1, Pallas kernels: 42.9 us -> 41.5 us  [on_device(): pl.pallas_call(functools.partial(kernel, sections, outer, inner), out_sha...]
where the time goes in v1:
time: 43.3 us; the launch traced here: 43.1 us
  Pallas kernels  41.5 us (96%)
  local copies, waits for them, and re-layouts  1.57 us (4%)
    pallas_call x1, Pallas kernels, on_device(): pl.pallas_call(functools.partial(kernel, sections, outer, inner), out_sha...  41.5 us
    unnamed x1, local copies, waits for them, and re-layouts  1.57 us

profile of v1, /device:TPU:1, one launch (start us, length us, event | category | flops | bytes accessed | tf_op | source)
XLA Modules:
  0.0 43.1 jit_solution(13082589780534758186)
XLA Ops:
  0.0 41.5 %section_attention.1 = bf16[8,8192]{1,0:T(8,128)(2,1)} custom-call(s32[4]{0:T(128)} %lengths_ref.1, bf16[8,8192]{1,0:T(8,128)(2,1)} %q_hbm.1, bf16[8,1024]{1,0:T(8,128)(2,1)} %nk_hbm.1, bf16[8,1024]{1,0:T(8,128)(2,1)} %nv_hbm.1, bf16[1024,1024]{1,0:T(8,128)(2,1)} %k_hbm.1, bf16[1024,1024]{1,0:T(8,128)(2,1)} %v_hbm.1), custom_call_target="tpu_custom_call" | custom-call | tf_op jit(solution)/shard_map/section_attention/pallas_call | solution.py:296
  41.5 1.6 %copy.8 = bf16[8,8192]{1,0:T(8,128)(2,1)} copy(bf16[8,8192]{1,0:T(8,128)(2,1)} %section_attention.1) | data formatting | bytes 262144

commit v2 on v1

--- a/solution.py
+++ b/solution.py
@@ -14,13 +14,20 @@
 LANES = 128
 NEG = -1e30
 HALVES = 2
-LAG = 1
+LAG = 2
 LOG2E = 1.4426950408889634
 MESH = pl.DeviceIdType.MESH
 F32 = jnp.float32
 BF16 = jnp.bfloat16
 
 
+def line_order(at, outer):
+    near = sorted(range(outer), key=lambda q: (abs(q - at), abs(2 * q + 1 - outer)))
+    if len(near) > 2 and 2 * at + 1 != outer:
+        near.sort(key=lambda q: 0 if q == at else 1 if q == at ^ 1 else 2 + abs(q - at))
+    return near
+
+
 def lane_of(stats, h):
     return jnp.broadcast_to(stats[:, h : h + 1], stats.shape)
 
@@ -29,7 +36,7 @@
     sections, outer, inner,
     lengths_ref, q_hbm, nk_hbm, nv_hbm, k_hbm, v_hbm, out_ref,
     nkbuf, nvbuf, kbuf, vbuf, qbuf, obuf, ostat, ybuf, ystat, cbuf, cstat, zbuf, zstat,
-    local_sem, qz_send, qy_send, qf_send, q_recv,
+    local_sem, qz_send, qr_send, qy_send, qf_send, q_recv,
     yo_send, ys_send, yo_recv, ys_recv, xo_send, xs_send, zo_send, zs_send, zo_recv, zs_recv,
 ):
     sec = lax.axis_index("section")
@@ -46,19 +53,16 @@
     def cut(hf):
         return pl.ds(hf * span, span)
 
+    table = [line_order(at, outer) for at in range(outer)]
+
     def outer_at(d):
-        if outer & (outer - 1):
-            return (a + d) % outer
-        at, bit = 0, 1
-        while bit < outer:
-            at = at + ((a // bit + d // bit) % 2) * bit
-            bit *= 2
+        at = table[0][d]
+        for k in range(1, outer):
+            at = jnp.where(a == k, table[k][d], at)
         return at
 
-    def outer_back(d):
-        if outer & (outer - 1):
-            return (a + outer - d) % outer
-        return outer_at(d)
+    def side_of(step):
+        return (a + step >= 0) & (a + step < outer)
 
     def inner_at(e):
         return (b + e) % inner
@@ -74,24 +78,35 @@
         load.start()
 
     barrier = pltpu.get_barrier_semaphore()
-    peers = [(sec, outer_at(d) * inner + b) for d in range(1, outer)]
-    peers += [(sec, a * inner + inner_at(e)) for e in range(1, inner)]
+    peers = [(sec, a * inner + inner_at(e)) for e in range(1, inner)]
     peers += [(following, me), (previous, me)]
     for s_at, k_at in peers:
         pl.semaphore_signal(
             barrier, inc=1, device_id={"section": s_at, "kv": k_at}, device_id_type=MESH
         )
-    pl.semaphore_wait(barrier, len(peers))
+    for step in (1, -1):
+
+        @pl.when(side_of(step))
+        def _(step=step):
+            pl.semaphore_signal(
+                barrier, inc=1, device_id={"section": sec, "kv": me + step * inner}, device_id_type=MESH
+            )
+
+    lines = side_of(1).astype(jnp.int32) + side_of(-1).astype(jnp.int32)
+    pl.semaphore_wait(barrier, len(peers) + lines)
 
     sends = []
 
-    def push(src, dst, send_sem, recv_sem, s_at, k_at):
+    def push(src, dst, send_sem, recv_sem, s_at, k_at, when=None):
         copy = pltpu.make_async_remote_copy(
             src_ref=src, dst_ref=dst, send_sem=send_sem, recv_sem=recv_sem,
             device_id={"section": s_at, "kv": k_at}, device_id_type=MESH,
         )
-        copy.start()
-        sends.append(copy)
+        if when is None:
+            copy.start()
+        else:
+            pl.when(when)(copy.start)
+        sends.append((copy, when))
 
     def arrived(dst, recv_sem):
         pltpu.make_async_copy(dst, dst, recv_sem).wait()
@@ -102,17 +117,24 @@
                 q_hbm.at[:, cut(hf)], qbuf.at[me, :, cut(hf)], qy_send.at[e, hf], q_recv.at[me, hf],
                 sec, a * inner + inner_at(e),
             )
-    for d in range(1, outer):
-        for hf in range(HALVES):
-            push(
-                q_hbm.at[:, cut(hf)], qbuf.at[me, :, cut(hf)], qz_send.at[d, hf], q_recv.at[me, hf],
-                sec, outer_at(d) * inner + b,
+    for hf in range(HALVES):
+        for i, step in enumerate((1, -1)):
+            push(
+                q_hbm.at[:, cut(hf)], qbuf.at[me, :, cut(hf)], qz_send.at[i, hf], q_recv.at[me, hf],
+                sec, jnp.clip(a + step, 0, outer - 1) * inner + b, side_of(step),
             )
 
     def forward(d, hf):
-        slot = outer_back(d) * inner + b
+        zs = outer_at(d)
+        slot = zs * inner + b
         piece = qbuf.at[slot, :, cut(hf)]
         arrived(piece, q_recv.at[slot, hf])
+        for i, step in enumerate((1, -1)):
+            onward = side_of(step) & (zs < a if step > 0 else zs > a)
+            push(
+                piece, piece, qr_send.at[d, i, hf], q_recv.at[slot, hf],
+                sec, jnp.clip(a + step, 0, outer - 1) * inner + b, onward,
+            )
         for e in range(1, inner):
             push(
                 piece, piece, qf_send.at[d, e, hf], q_recv.at[slot, hf], sec, a * inner + inner_at(e)
@@ -248,23 +270,33 @@
     pad = jnp.zeros((LANES - rows, kbuf.shape[1]), F32)
     kbuf[pl.ds(depth, LANES), :] = jnp.concatenate([nkbuf[...].astype(F32), pad], 0).astype(BF16)
     vbuf[pl.ds(depth, LANES), :] = jnp.concatenate([nvbuf[...].astype(F32), pad], 0).astype(BF16)
-    steps = [(d, hf) for d in range(outer) for hf in range(HALVES)]
-    for t, (d, hf) in enumerate(steps):
-        zc = outer_back(d)
-        if t + 1 < len(steps) and steps[t + 1][0] > 0:
-            forward(*steps[t + 1])
+    work = []
+    for d in range(1, outer):
+        work += [(forward, d, hf) for hf in range(HALVES)]
+        if d <= HALVES:
+            work.append((None, 0, d - 1))
+    work += [(None, 0, hf) for hf in range(outer - 1, HALVES)]
+    for d in [*range(2, outer), 1]:
+        work += [(None, d, hf) for hf in range(HALVES)]
+    done = []
+    for act, d, hf in work:
+        if act is not None:
+            act(d, hf)
+            continue
+        zc = outer_at(d)
         for e in range(1, inner):
             slot = zc * inner + inner_at(e)
             arrived(qbuf.at[slot, :, cut(hf)], q_recv.at[slot, hf])
         compute(zc, hf)
         if d > 0:
             spread(zc, hf)
-        if t >= LAG and steps[t - LAG][0] > 0:
-            combine(outer_back(steps[t - LAG][0]), steps[t - LAG][1])
+            done.append((zc, hf))
+            if len(done) > LAG:
+                combine(*done.pop(0))
     for hf in range(HALVES):
         deliver(hf)
-    for d, hf in steps[len(steps) - LAG :]:
-        combine(outer_back(d), hf)
+    for zc, hf in done:
+        combine(zc, hf)
 
     def store_out(cols, value):
         out_ref[:, cols] = value
@@ -277,8 +309,11 @@
         mix(
             hf, [zbuf.at[at] for at in origins], [zstat[at, hf] for at in origins], store_out
         )
-    for copy in sends:
-        copy.wait_send()
+    for copy, when in sends:
+        if when is None:
+            copy.wait_send()
+        else:
+            pl.when(when)(copy.wait_send)
 
 
 def split_of(count):
@@ -313,7 +348,8 @@
             pltpu.VMEM((outer + inner, rows, width), BF16),
             pltpu.VMEM((outer + inner, HALVES, rows, LANES), F32),
             dma((5,)),
-            dma((outer, HALVES)),
+            dma((2, HALVES)),
+            dma((outer, 2, HALVES)),
             dma((inner, HALVES)),
             dma((outer, inner, HALVES)),
             dma((count, HALVES)),

time: 43.3 us -> 40.3 us (0.931)
  Pallas kernels: 41.5 us -> 38.5 us
    pallas_call x1, Pallas kernels: 41.5 us -> 38.5 us  [on_device(): pl.pallas_call(functools.partial(kernel, sections, outer, inner), out_sha...]
where the time goes in v2:
time: 40.3 us; the launch traced here: 40.1 us
  Pallas kernels  38.5 us (96%)
  local copies, waits for them, and re-layouts  1.57 us (4%)
    pallas_call x1, Pallas kernels, on_device(): pl.pallas_call(functools.partial(kernel, sections, outer, inner), out_sha...  38.5 us
    unnamed x1, local copies, waits for them, and re-layouts  1.57 us

profile of v2, /device:TPU:1, one launch (start us, length us, event | category | flops | bytes accessed | tf_op | source)
XLA Modules:
  0.0 40.1 jit_solution(11190596515244922649)
XLA Ops:
  0.0 38.5 %section_attention.1 = bf16[8,8192]{1,0:T(8,128)(2,1)} custom-call(s32[4]{0:T(128)} %lengths_ref.1, bf16[8,8192]{1,0:T(8,128)(2,1)} %q_hbm.1, bf16[8,1024]{1,0:T(8,128)(2,1)} %nk_hbm.1, bf16[8,1024]{1,0:T(8,128)(2,1)} %nv_hbm.1, bf16[1024,1024]{1,0:T(8,128)(2,1)} %k_hbm.1, bf16[1024,1024]{1,0:T(8,128)(2,1)} %v_hbm.1), custom_call_target="tpu_custom_call" | custom-call | tf_op jit(solution)/shard_map/section_attention/pallas_call | solution.py:331
  38.5 1.6 %copy.8 = bf16[8,8192]{1,0:T(8,128)(2,1)} copy(bf16[8,8192]{1,0:T(8,128)(2,1)} %section_attention.1) | data formatting | bytes 262144

commit v3 on v2

--- a/solution.py
+++ b/solution.py
@@ -265,24 +265,30 @@
             following, target,
         )
 
-    for load in loads:
-        load.wait()
-    pad = jnp.zeros((LANES - rows, kbuf.shape[1]), F32)
-    kbuf[pl.ds(depth, LANES), :] = jnp.concatenate([nkbuf[...].astype(F32), pad], 0).astype(BF16)
-    vbuf[pl.ds(depth, LANES), :] = jnp.concatenate([nvbuf[...].astype(F32), pad], 0).astype(BF16)
+    def settle():
+        for load in loads:
+            load.wait()
+        pad = jnp.zeros((LANES - rows, kbuf.shape[1]), F32)
+        kbuf[pl.ds(depth, LANES), :] = jnp.concatenate([nkbuf[...].astype(F32), pad], 0).astype(BF16)
+        vbuf[pl.ds(depth, LANES), :] = jnp.concatenate([nvbuf[...].astype(F32), pad], 0).astype(BF16)
+
     work = []
     for d in range(1, outer):
         work += [(forward, d, hf) for hf in range(HALVES)]
         if d <= HALVES:
             work.append((None, 0, d - 1))
     work += [(None, 0, hf) for hf in range(outer - 1, HALVES)]
-    for d in [*range(2, outer), 1]:
-        work += [(None, d, hf) for hf in range(HALVES)]
+    work += [(None, d, hf) for hf in range(HALVES) for d in range(2, outer)]
+    work += [(None, 1, hf) for hf in range(HALVES)]
     done = []
+    settled = False
     for act, d, hf in work:
         if act is not None:
             act(d, hf)
             continue
+        if not settled:
+            settle()
+            settled = True
         zc = outer_at(d)
         for e in range(1, inner):
             slot = zc * inner + inner_at(e)

time: 40.3 us -> 39.8 us (0.988)
    pallas_call x1, Pallas kernels: 38.5 us -> 38.1 us  [on_device(): pl.pallas_call(functools.partial(kernel, sections, outer, inner), out_sha...]
where the time goes in v3:
time: 39.8 us; the launch traced here: 39.7 us
  Pallas kernels  38.1 us (96%)
  local copies, waits for them, and re-layouts  1.57 us (4%)
    pallas_call x1, Pallas kernels, on_device(): pl.pallas_call(functools.partial(kernel, sections, outer, inner), out_sha...  38.1 us
    unnamed x1, local copies, waits for them, and re-layouts  1.57 us

profile of v3, /device:TPU:1, one launch (start us, length us, event | category | flops | bytes accessed | tf_op | source)
XLA Modules:
  0.0 39.7 jit_solution(5442801627479581712)
XLA Ops:
  0.0 38.1 %section_attention.1 = bf16[8,8192]{1,0:T(8,128)(2,1)} custom-call(s32[4]{0:T(128)} %lengths_ref.1, bf16[8,8192]{1,0:T(8,128)(2,1)} %q_hbm.1, bf16[8,1024]{1,0:T(8,128)(2,1)} %nk_hbm.1, bf16[8,1024]{1,0:T(8,128)(2,1)} %nv_hbm.1, bf16[1024,1024]{1,0:T(8,128)(2,1)} %k_hbm.1, bf16[1024,1024]{1,0:T(8,128)(2,1)} %v_hbm.1), custom_call_target="tpu_custom_call" | custom-call | tf_op jit(solution)/shard_map/section_attention/pallas_call | solution.py:337
  38.1 1.6 %copy.8 = bf16[8,8192]{1,0:T(8,128)(2,1)} copy(bf16[8,8192]{1,0:T(8,128)(2,1)} %section_attention.1) | data formatting | bytes 262144
